TPU v7x, 128 devices: a whole 4x4x4 slice. The times are simulated.
128 devices in a mesh: tm: 8 (over y, x_hi), agent: 16 (over z, x_lo, core).
Axes of the slice: x: 4 (x_hi: 2, x_lo: 2; x = x_hi * 2 + x_lo), y: 4, z: 4, core: 2. Of those that a mesh axis runs over, the one named last changes fastest.
Arguments:
- tokens: bfloat16 [32, 1024, 1024], P('tm', 'agent'), may hold values from -6 to 6
- conv_taps: float32 [5, 1024], replicated, may hold values from -3 to 3
- norm_first: float32 [1024], replicated, may hold values from 0.1 to 1.9
- norm_second: float32 [1024], replicated, may hold values from 0.1 to 1.9
- norm_third: float32 [1024], replicated, may hold values from 0.1 to 1.9
- w_in: bfloat16 [1024, 3072], replicated, may hold values from -0.1875 to 0.1875
- w_out: bfloat16 [3072, 1024], replicated, may hold values from -0.109375 to 0.109375
- w_query: bfloat16 [1024, 1024], replicated, may hold values from -16 to 16
- w_key: bfloat16 [1024, 1024], replicated, may hold values from -16 to 16
- w_value: bfloat16 [1024, 1024], replicated, may hold values from -0.1875 to 0.1875
- w_output: bfloat16 [1024, 1024], replicated, may hold values from -0.1875 to 0.1875
- agent_order: int32 [1024], P('agent'), may hold values from 0 to 1023, each once
- present_steps: int32 [1024], P('agent'), may hold values from 1 to 32
Outputs:
- result: bfloat16 [32, 1024, 1024], P('tm', 'agent')
Inputs may be any that keep to these rules, and one draw needn't show every extreme that they name: `agent_order`: each of 0 to 1023 appears once.
All inputs are finite; a program needn't handle non-finite values.
Results may differ from a plain program's by a relative error of at most 0.012.
Values may be sent and summed in bfloat16 or wider, within the bound.
A program may use at most 192 MiB of HBM per device.

v0:
```python
import jax
import jax.numpy as jnp
from jax import lax
from jax.sharding import PartitionSpec as P

HEADS = 16
EPS = 1e-05


def shifted(shard, axis, by):
    count = lax.axis_size(axis)
    pairs = [(i, i + by) for i in range(count) if 0 <= i + by < count]
    return lax.ppermute(shard, axis, pairs)


def normed_rows(rows, gain):
    values = rows.astype(jnp.float32)
    scale = lax.rsqrt(jnp.mean(values * values, axis=-1, keepdims=True) + EPS)
    return values * scale * gain


def make_absorb(query, own_order, steps, heads_here, project):
    step_count, agent_count, width = query.shape
    head_size = width // heads_here
    scale = head_size ** (-0.5)
    split_query = query.reshape(step_count, agent_count, heads_here, head_size)
    init = (
        jnp.full((step_count, heads_here, agent_count), -1e30, jnp.float32),
        jnp.zeros((step_count, heads_here, agent_count), jnp.float32),
        jnp.zeros((step_count, agent_count, heads_here, head_size), jnp.float32),
    )

    def absorb(carry, piece, start):
        best, total, summed = carry
        key_piece, value_piece, order_piece, present_piece = project(piece)
        count = key_piece.shape[1]
        key_piece = key_piece.reshape(step_count, count, heads_here, head_size)
        value_piece = value_piece.reshape(step_count, count, heads_here, head_size)
        scores = (
            jnp.einsum(
                "sahd,sbhd->shab", split_query, key_piece, preferred_element_type=jnp.float32
            )
            * scale
        )
        other_order = order_piece[0]
        earlier = other_order[None, None, :] < own_order[None, :, None]
        alive = steps[:, None, None] < present_piece[0][None, None, :]
        itself = other_order[None, None, :] == own_order[None, :, None]
        visible = (earlier & alive | itself)[:, None]
        masked = jnp.where(visible, scores, -1e30)
        fresh = jnp.maximum(best, jnp.max(masked, axis=-1))
        weights = jnp.where(visible, jnp.exp(masked - fresh[..., None]), 0.0).astype(jnp.bfloat16)
        total = jnp.sum(weights.astype(jnp.float32), axis=-1)
        part_sum = jnp.einsum(
            "shab,sbhd->sahd", weights, value_piece, preferred_element_type=jnp.float32
        )
        summed = part_sum
        return (fresh, total, summed)

    return (absorb, init)


def finish(carry, shape):
    best, total, summed = carry
    attended = summed / jnp.transpose(total, (0, 2, 1))[..., None]
    return attended.astype(jnp.bfloat16).reshape(shape)


def identity_piece(piece):
    return piece


def per_device(
    tokens,
    conv_taps,
    norm_first,
    norm_second,
    norm_third,
    w_in,
    w_out,
    w_query,
    w_key,
    w_value,
    w_output,
    agent_order,
    present_steps,
):
    step_count, agent_count, width = tokens.shape
    reach = conv_taps.shape[0] - 1
    earlier_steps = shifted(tokens, "tm", 1)
    extended = normed_rows(jnp.concatenate([earlier_steps, tokens], axis=0), norm_first)
    mixed = jnp.zeros((step_count, agent_count, width), jnp.float32)
    for lag in range(reach + 1):
        mixed = mixed + conv_taps[lag] * extended[reach - lag : reach - lag + step_count]
    first = (tokens.astype(jnp.float32) + mixed).astype(jnp.bfloat16)
    flat = first.reshape(step_count * agent_count, width)
    inner = normed_rows(flat, norm_second).astype(jnp.bfloat16)
    hidden = jax.nn.gelu(
        jnp.dot(inner, w_in, preferred_element_type=jnp.float32), approximate=False
    ).astype(jnp.bfloat16)
    second = (
        flat.astype(jnp.float32) + jnp.dot(hidden, w_out, preferred_element_type=jnp.float32)
    ).astype(jnp.bfloat16)
    attn_in = normed_rows(second, norm_third).astype(jnp.bfloat16)
    query = (
        jnp.dot(attn_in, w_query, preferred_element_type=jnp.float32)
        .astype(jnp.bfloat16)
        .reshape(step_count, agent_count, width)
    )
    order_rows = agent_order.reshape(1, agent_count)
    present_rows = present_steps.reshape(1, agent_count)
    keys = (
        jnp.dot(attn_in, w_key, preferred_element_type=jnp.float32)
        .astype(jnp.bfloat16)
        .reshape(step_count, agent_count, width)
    )
    values = (
        jnp.dot(attn_in, w_value, preferred_element_type=jnp.float32)
        .astype(jnp.bfloat16)
        .reshape(step_count, agent_count, width)
    )
    keys, values = (keys, values)
    query, keys, values = (
        lax.all_to_all(query, "tm", split_axis=2, concat_axis=0, tiled=True),
        lax.all_to_all(keys, "tm", split_axis=2, concat_axis=0, tiled=True),
        lax.all_to_all(values, "tm", split_axis=2, concat_axis=0, tiled=True),
    )
    steps = jnp.arange(query.shape[0], dtype=jnp.int32)
    heads_here = HEADS // lax.axis_size("tm")
    absorb, init = make_absorb(query, agent_order, steps, heads_here, identity_piece)
    carry = absorb(
        init,
        (
            lax.all_gather(keys, "agent", axis=1, tiled=True),
            lax.all_gather(values, "agent", axis=1, tiled=True),
            lax.all_gather(order_rows, "agent", axis=1, tiled=True),
            lax.all_gather(present_rows, "agent", axis=1, tiled=True),
        ),
        jnp.int32(0),
    )
    attended = finish(carry, query.shape)
    attended = lax.all_to_all(attended, "tm", split_axis=0, concat_axis=2, tiled=True)
    projected = jnp.dot(
        attended.reshape(step_count * agent_count, width),
        w_output,
        preferred_element_type=jnp.float32,
    )
    result = second.astype(jnp.float32) + projected
    return result.astype(jnp.bfloat16).reshape(step_count, agent_count, width)


def solution(mesh):
    in_specs = (
        P("tm", "agent", None),
        P(),
        P(),
        P(),
        P(),
        P(),
        P(),
        P(),
        P(),
        P(),
        P(),
        P("agent"),
        P("agent"),
    )
    out_specs = P("tm", "agent", None)
    return jax.shard_map(
        per_device, mesh=mesh, in_specs=in_specs, out_specs=out_specs, check_vma=False
    )
```

profile of v0, /device:TPU:0, one launch (start us, length us, event | category | flops | bytes accessed | tf_op | source)
XLA Modules:
  0.0 235.1 jit_solution(14129081017646608805)
XLA Ops:
  6.5 5.3 %collective-permute-start = (bf16[4,64,1024]{2,1,0:T(8,128)(2,1)}, bf16[4,64,1024]{2,1,0:T(8,128)(2,1)S(1)}, u32[]{:S(2)}, u32[]{:S(2)}) collective-permute-start(bf16[4,64,1024]{2,1,0:T(8,128)(2,1)} %param.13), channel_id=1, source_target_pairs={{0,16},{16,32},{32,48},{48,64},{64,80},{80,96},{96,112},{1,17},{17... | collective-permute-start | bytes 1572872 | tf_op jit(solution)/shard_map/ppermute | solution.py:13
  12.8 10.5 %collective-permute-done = bf16[4,64,1024]{2,1,0:T(8,128)(2,1)S(1)} collective-permute-done((bf16[4,64,1024]{2,1,0:T(8,128)(2,1)}, bf16[4,64,1024]{2,1,0:T(8,128)(2,1)S(1)}, u32[]{:S(2)}, u32[]{:S(2)}) %collective-permute-start) | collective-permute-done | bytes 524320 | tf_op jit(solution)/shard_map/ppermute | solution.py:13
  26.9 15.0 %fusion.53 = (f32[256]{0:T(256)S(1)}, bf16[256,1024]{1,0:T(8,128)(2,1)}) fusion(bf16[3072,1024]{1,0:T(8,128)(2,1)} %param.19, bf16[256,1024]{1,0:T(8,128)(2,1)S(1)} %fusion.63, bf16[1024,3072]{1,0:T(8,128)(2,1)} %param.18, bf16[256,1024]{1,0:T(8,128)(2,1)S(1)} %bitcast.69), kind=kOutput, calls=%fused_computation.70 | convolution fusion | flops 3273916160 | bytes 14156800 | tf_op jit(solution)/shard_map/dot_general | solution.py:102
  41.9 1.8 convolution_convert_fusion
  45.4 18.3 %all_to_all.66 = bf16[8,2,16384]{2,1,0:T(2,128)(2,1)S(1)} all-to-all(bf16[8,2,16384]{2,1,0:T(2,128)(2,1)S(1)} %reshape.197), channel_id=1, replica_groups=mesh['tm'=8,'agent'=16] {'tm'}, dimensions={0} | all-to-all | bytes 1048576 | tf_op jit(solution)/shard_map/all_to_all | solution.py:125
  65.8 2.4 %convolution_convert_fusion.2 = bf16[256,1024]{1,0:T(8,128)(2,1)S(1)} fusion(bf16[1024,1024]{1,0:T(8,128)(2,1)} %param.22, bf16[256,1024]{1,0:T(8,128)(2,1)S(1)} %copy-done.8, f32[1024]{0:T(1024)S(1)} %copy-done.5, f32[256]{0:T(256)S(1)} %add_rsqrt_fusion.2), kind=kOutput, calls=%fused_computation.68 | convolution fusion | flops 538181632 | bytes 3150848 | tf_op jit(solution)/shard_map/dot_general | solution.py:118
  69.6 17.9 %all_to_all.67 = bf16[8,2,16384]{2,1,0:T(2,128)(2,1)S(1)} all-to-all(bf16[8,2,16384]{2,1,0:T(2,128)(2,1)S(1)} %reshape.195), channel_id=1, replica_groups=mesh['tm'=8,'agent'=16] {'tm'}, dimensions={0} | all-to-all | bytes 1048576 | tf_op jit(solution)/shard_map/all_to_all | solution.py:126
  91.4 14.2 %all-reduce.2 = (s32[1024]{0:T(1024)S(1)}, s32[1024]{0:T(1024)S(1)}) all-reduce(s32[1024]{0:T(1024)S(1)} %dynamic-update-slice, s32[1024]{0:T(1024)S(1)} %dynamic-update-slice.1), channel_id=2, replica_groups=mesh['tm'=8,'agent'=16] {'agent'}, use_global_device_ids=true, to_apply=%add | all-reduce | flops 2048 | bytes 16384
  105.9 2.4 %convolution_convert_fusion.1 = bf16[256,1024]{1,0:T(8,128)(2,1)S(1)} fusion(bf16[1024,1024]{1,0:T(8,128)(2,1)} %param.20, bf16[256,1024]{1,0:T(8,128)(2,1)S(1)} %copy-done.8, f32[1024]{0:T(1024)S(1)} %copy-done.5, f32[256]{0:T(256)S(1)} %add_rsqrt_fusion.2), kind=kOutput, calls=%fused_computation.67 | convolution fusion | flops 538181632 | bytes 3150848 | tf_op jit(solution)/shard_map/dot_general | solution.py:106
  109.0 1.5 reshape.199
  110.5 4.4 %all-to-all-start.1 = ((bf16[8,2,16384]{2,1,0:T(2,128)(2,1)}), bf16[8,2,16384]{2,1,0:T(2,128)(2,1)}, u32[]{:S(2)}, u32[]{:S(2)}) async-start(bf16[8,2,16384]{2,1,0:T(2,128)(2,1)} %reshape.199), calls=%async_computation.1 | async-start | bytes 1048576 | tf_op jit(solution)/shard_map/all_to_all | solution.py:124
  114.9 1.4 and_or_fusion
  116.3 10.8 %all-to-all-done.1 = bf16[8,2,16384]{2,1,0:T(2,128)(2,1)} async-done(((bf16[8,2,16384]{2,1,0:T(2,128)(2,1)}), bf16[8,2,16384]{2,1,0:T(2,128)(2,1)}, u32[]{:S(2)}, u32[]{:S(2)}) %all-to-all-start.1) | async-done | bytes 524320 | tf_op jit(solution)/shard_map/all_to_all | solution.py:124
  127.1 2.7 %reshape.200 = bf16[1024,4,64]{2,1,0:T(4,128)(2,1)S(1)} reshape(bf16[8,2,16384]{2,1,0:T(2,128)(2,1)} %all-to-all-done.1) | data formatting | bytes 1048576
  131.0 2.4 %reshape.174 = bf16[32,64,2,64]{3,2,1,0:T(2,128)(2,1)S(1)} reshape(bf16[8,4,64,128]{3,2,1,0:T(8,128)(2,1)} %bitcast.70) | data formatting | bytes 1048576 | tf_op jit(solution)/shard_map/reshape | solution.py:26
  133.5 12.5 %copy.33 = bf16[32,1024,128]{1,2,0:T(8,128)(2,1)} copy(bf16[32,1024,128]{2,0,1:T(8,128)(2,1)} %all-gather.7.cloned.1.call-done) | data formatting | bytes 16777216 | tf_op jit(solution)/shard_map/all_gather | solution.py:134
  146.0 10.3 %fusion = (f32[32,2,64]{2,1,0:T(2,128)S(1)}, f32[32,2,64,1024]{3,2,1,0:T(8,128)}) fusion(pred[32,64,1024]{2,1,0:T(8,128)(4,1)S(1)} %and_or_fusion, bf16[32,1024,2,64]{1,3,2,0:T(8,128)(2,1)} %bitcast.61, bf16[32,64,2,64]{3,2,1,0:T(2,128)(2,1)S(1)} %reshape.174), kind=kOutput, calls=%fused_computation.3 | convolution fusion | flops 549449728 | bytes 27803648 | tf_op jit(solution)/shard_map/sahd,sbhd->shab/dot_general | solution.py:40
  156.3 9.0 %convert_reduce_fusion = f32[32,2,64]{2,1,0:T(2,128)S(1)} fusion(f32[32,2,64]{2,1,0:T(2,128)S(1)} %broadcast_maximum_fusion, f32[32,2,64,1024]{3,2,1,0:T(8,128)} %get-tuple-element.19, pred[32,64,1024]{2,1,0:T(8,128)(4,1)S(1)} %and_or_fusion), kind=kLoop, calls=%fused_computation | loop fusion | flops 29356032 | bytes 18907136 | tf_op jit(solution)/shard_map/reduce_sum | solution.py:53
  165.3 15.4 %all-gather.5.cloned.1.call-done = bf16[32,1024,128]{2,0,1:T(8,128)(2,1)} async-done(((bf16[32,64,128]{2,0,1:T(8,128)(2,1)}), bf16[32,1024,128]{2,0,1:T(8,128)(2,1)}) %all-gather.5.cloned.1.call-update) | async-done | bytes 8388624 | tf_op jit(solution)/shard_map/all_gather | solution.py:135
  180.7 12.2 %copy.27 = bf16[32,1024,128]{1,2,0:T(8,128)(2,1)} copy(bf16[32,1024,128]{2,0,1:T(8,128)(2,1)} %all-gather.5.cloned.1.call-done) | data formatting | bytes 16777216 | tf_op jit(solution)/shard_map/all_gather | solution.py:135
  192.9 11.7 %fusion.13 = bf16[32,64,2,64]{1,3,2,0:T(8,128)(2,1)} fusion(bf16[32,1024,2,64]{1,3,2,0:T(8,128)(2,1)} %bitcast.62, f32[32,64,2]{1,2,0:T(2,128)S(1)} %bitcast.79, f32[32,2,64,1024]{3,2,1,0:T(8,128)} %get-tuple-element.19, f32[32,2,64]{2,1,0:T(2,128)S(1)} %broadcast_maximum_fusion, pred[32,64,1024]{2,1,0:T(8,128)(4,1)S(1)} %and_or_fusion), kind=kOutput, calls=%fused_computation.29 | convolution fusion | flops 558366720 | bytes 27820032 | tf_op jit(solution)/shard_map/shab,sbhd->sahd/dot_general | solution.py:54
  204.6 1.7 copy.35
  206.3 18.5 %all_to_all.68 = bf16[32,64,128]{2,1,0:T(8,128)(2,1)S(1)} all-to-all(bf16[32,64,128]{2,1,0:T(8,128)(2,1)S(1)} %copy.35), channel_id=1, replica_groups=mesh['tm'=8,'agent'=16] {'tm'}, dimensions={0} | all-to-all | bytes 1048576 | tf_op jit(solution)/shard_map/all_to_all | solution.py:142
  225.2 3.1 %fusion.49 = bf16[256,1024]{1,0:T(8,128)(2,1)} fusion(bf16[1024,1024]{1,0:T(8,128)(2,1)} %param.23, bf16[256,1024]{1,0:T(8,128)(2,1)S(1)} %copy-done.9, bf16[32,8,8,128]{3,2,1,0:T(8,128)(2,1)S(1)} %bitcast.78), kind=kOutput, calls=%fused_computation.65 | convolution fusion | flops 537657344 | bytes 3670016 | tf_op jit(solution)/shard_map/dot_general | solution.py:143
  (53 shorter events, 15.3 us)
Async XLA Ops:
  6.5 35.4 %copy-start = (bf16[1024,1024]{1,0:T(8,128)(2,1)S(1)}, bf16[1024,1024]{1,0:T(8,128)(2,1)}, u32[]{:S(2)}) copy-start(bf16[1024,1024]{1,0:T(8,128)(2,1)} %param.21) | copy-start | bytes 6291460
  6.5 19.4 %copy-start.2 = (bf16[4,64,1024]{2,1,0:T(8,128)(2,1)S(1)}, bf16[4,64,1024]{2,1,0:T(8,128)(2,1)}, u32[]{:S(2)}) copy-start(bf16[4,64,1024]{2,1,0:T(8,128)(2,1)} %param.13) | copy-start | bytes 1572868
  6.5 127.0 %all-gather.7.cloned.1.call-start = ((), (), s32[]{:S(2)}) async-start(), calls=%async_computation.5 | async-start | bytes 8912896 | tf_op jit(solution)/shard_map/all_gather | solution.py:134
  6.5 16.8 %collective-permute-start = (bf16[4,64,1024]{2,1,0:T(8,128)(2,1)}, bf16[4,64,1024]{2,1,0:T(8,128)(2,1)S(1)}, u32[]{:S(2)}, u32[]{:S(2)}) collective-permute-start(bf16[4,64,1024]{2,1,0:T(8,128)(2,1)} %param.13), channel_id=1, source_target_pairs={{0,16},{16,32},{32,48},{48,64},{64,80},{80,96},{96,112},{1,17},{17... | collective-permute-start | bytes 1572872 | tf_op jit(solution)/shard_map/ppermute | solution.py:13
  26.0 0.7 copy-start.3
  26.9 15.1 %copy-start.5 = (f32[1024]{0:T(1024)S(1)}, f32[1024]{0:T(1024)}, u32[]{:S(2)}) copy-start(f32[1024]{0:T(1024)} %param.17) | copy-start | bytes 12292
  44.6 21.1 %copy-start.8 = (bf16[256,1024]{1,0:T(8,128)(2,1)S(1)}, bf16[256,1024]{1,0:T(8,128)(2,1)}, u32[]{:S(2)}) copy-start(bf16[256,1024]{1,0:T(8,128)(2,1)} %get-tuple-element.17) | copy-start | bytes 1572868
  65.7 114.9 %all-gather.5.cloned.1.call-start = ((), (), s32[]{:S(2)}) async-start(), calls=%async_computation.4 | async-start | bytes 8912896 | tf_op jit(solution)/shard_map/all_gather | solution.py:135
  68.9 20.7 %copy-start.7 = (u32[128]{0:T(128)S(1)}, u32[128]{0:T(128)}, u32[]{:S(2)}) copy-start(u32[128]{0:T(128)} %constant.80) | copy-start | bytes 1540
  68.9 22.1 %copy-start.4 = (s32[64]{0:T(128)S(1)}, s32[64]{0:T(128)}, u32[]{:S(2)}) copy-start(s32[64]{0:T(128)} %param.24) | copy-start | bytes 772
  68.9 22.3 %copy-start.6 = (s32[64]{0:T(128)S(1)}, s32[64]{0:T(128)}, u32[]{:S(2)}) copy-start(s32[64]{0:T(128)} %param.25) | copy-start | bytes 772
  110.5 16.5 %all-to-all-start.1 = ((bf16[8,2,16384]{2,1,0:T(2,128)(2,1)}), bf16[8,2,16384]{2,1,0:T(2,128)(2,1)}, u32[]{:S(2)}, u32[]{:S(2)}) async-start(bf16[8,2,16384]{2,1,0:T(2,128)(2,1)} %reshape.199), calls=%async_computation.1 | async-start | bytes 1048576 | tf_op jit(solution)/shard_map/all_to_all | solution.py:124
  204.6 20.6 %copy-start.9 = (bf16[256,1024]{1,0:T(8,128)(2,1)S(1)}, bf16[256,1024]{1,0:T(8,128)(2,1)}, u32[]{:S(2)}) copy-start(bf16[256,1024]{1,0:T(8,128)(2,1)} %get-tuple-element.17) | copy-start | bytes 1572868
  204.6 23.7 %copy-start.1 = (bf16[1024,1024]{1,0:T(8,128)(2,1)S(1)}, bf16[1024,1024]{1,0:T(8,128)(2,1)}, u32[]{:S(2)}) copy-start(bf16[1024,1024]{1,0:T(8,128)(2,1)} %param.21) | copy-start | bytes 6291460
Sparse Core Ops, SparseCore 0:
  65.8 53.2 all-gather.6
  120.8 59.7 all-gather.4
where the time goes:
time: 236 us; the launch traced here: 235 us
  blocking collectives  69 us (29%)
  matrix products  46.8 us (20%)
  local copies, waits for them, and re-layouts  44.6 us (19%)
  waiting for transfers between devices  36.7 us (16%)
  between operations  14.4 us (6%)
  other arithmetic  14 us (6%)
  starting transfers between devices  9.7 us (4%)
    all_to_all x1, blocking collectives, per_device(): lax.all_to_all(attended, 'tm', split_axis=0, concat_axis=2, tiled=True)  18.5 us
    all_to_all x1, blocking collectives, per_device(): lax.all_to_all(keys, 'tm', split_axis=2, concat_axis=0, tiled=True)  18.3 us
    all_to_all x1, blocking collectives, per_device(): lax.all_to_all(values, 'tm', split_axis=2, concat_axis=0, tiled=True)  17.9 us
    all_gather x1, waiting for transfers between devices, per_device(): lax.all_gather(values, 'agent', axis=1, tiled=True)  15.4 us
    dot_general x1, matrix products, per_device(): jnp.dot(hidden, w_out, preferred_element_type=jnp.float32)  15 us
    unnamed x1, blocking collectives  14.2 us
    all_gather x1, local copies, waits for them, and re-layouts, per_device(): lax.all_gather(keys, 'agent', axis=1, tiled=True)  12.5 us
    all_gather x1, local copies, waits for them, and re-layouts, per_device(): lax.all_gather(values, 'agent', axis=1, tiled=True)  12.2 us
  transfers between devices with their start and end apart: 4, of which 3 were waited for; matrix products, arithmetic and copies ran while one was open for 22% of the time, Pallas kernels for 0%

commit v1 on v0

--- a/solution.py
+++ b/solution.py
@@ -2,6 +2,7 @@
 import jax.numpy as jnp
 from jax import lax
 from jax.sharding import PartitionSpec as P
+from jax.lax import all_to_all, axis_size
 
 HEADS = 16
 EPS = 1e-05
@@ -131,7 +132,7 @@
     carry = absorb(
         init,
         (
-            lax.all_gather(keys, "agent", axis=1, tiled=True),
+            jnp.concatenate(all_to_all(jnp.stack([keys] * axis_size("agent")), "agent", 0, 0), 1),
             lax.all_gather(values, "agent", axis=1, tiled=True),
             lax.all_gather(order_rows, "agent", axis=1, tiled=True),
             lax.all_gather(present_rows, "agent", axis=1, tiled=True),

time: 236 us -> 353 us (1.50)
  blocking collectives: 69 us -> 139 us
  local copies, waits for them, and re-layouts: 44.6 us -> 79 us
  starting transfers between devices: 9.7 us -> 19.2 us
    unnamed x1, blocking collectives: 14.2 us -> 99.1 us
    another operation x0 -> x2, local copies, waits for them, and re-layouts: none -> 28 us  [the longest x1 22.6 us: absorb(): key_piece = key_piece.reshape(step_count, count, heads_here, head_size)]
    reshape x0 -> x1, local copies, waits for them, and re-layouts: none -> 18.7 us  [per_device(): jnp.concatenate(all_to_all(jnp.stack([keys] * axis_size('agent')), 'agent...]
    all_to_all x1 -> x0, blocking collectives: 18.3 us -> none  [per_device(): lax.all_to_all(keys, 'tm', split_axis=2, concat_axis=0, tiled=True)]
    all_gather x1, waiting for transfers between devices: 15.4 us -> 0.02 us  [per_device(): lax.all_gather(values, 'agent', axis=1, tiled=True)]
    all_gather x1 -> x0, local copies, waits for them, and re-layouts: 12.5 us -> none  [per_device(): lax.all_gather(keys, 'agent', axis=1, tiled=True)]
    all_to_all x0 -> x2, waiting for transfers between devices: none -> 12 us  [the longest x1 12 us: per_device(): lax.all_to_all(keys, 'tm', split_axis=2, concat_axis=0, tiled=True)]
    all_to_all x0 -> x2, starting transfers between devices: none -> 10.4 us  [the longest x1 6.88 us: per_device(): all_to_all(jnp.stack([keys] * axis_size('agent')), 'agent', 0, 0)]
  transfers between devices with their start and end apart: 4 -> 5, of which waited for: 3 -> 3; matrix products, arithmetic and copies ran while one was open for 22% -> 25% of each run, Pallas kernels for 0% -> 0%
where the time goes in v1:
time: 353 us; the launch traced here: 349 us
  blocking collectives  139 us (39%)
  local copies, waits for them, and re-layouts  79 us (22%)
  matrix products  46.4 us (13%)
  waiting for transfers between devices  37.7 us (11%)
  starting transfers between devices  19.2 us (5%)
  between operations  14.3 us (4%)
  other arithmetic  13.9 us (4%)
    unnamed x1, blocking collectives  99.1 us
    another operation x1, local copies, waits for them, and re-layouts, absorb(): key_piece = key_piece.reshape(step_count, count, heads_here, head_size)  22.6 us
    all_to_all x1, blocking collectives, per_device(): lax.all_to_all(attended, 'tm', split_axis=0, concat_axis=2, tiled=True)  21.5 us
    reshape x1, local copies, waits for them, and re-layouts, per_device(): jnp.concatenate(all_to_all(jnp.stack([keys] * axis_size('agent')), 'agent...  18.7 us
    all_to_all x1, blocking collectives, per_device(): lax.all_to_all(values, 'tm', split_axis=2, concat_axis=0, tiled=True)  18.3 us
    all_to_all x1, waiting for transfers between devices, per_device(): lax.all_to_all(query, 'tm', split_axis=2, concat_axis=0, tiled=True)  15.1 us
    dot_general x1, matrix products, per_device(): jnp.dot(hidden, w_out, preferred_element_type=jnp.float32)  15 us
    all_gather x1, local copies, waits for them, and re-layouts, per_device(): lax.all_gather(values, 'agent', axis=1, tiled=True)  12.2 us
  transfers between devices with their start and end apart: 5, of which 3 were waited for; matrix products, arithmetic and copies ran while one was open for 25% of the time, Pallas kernels for 0%

profile of v1, /device:TPU:0, one launch (start us, length us, event | category | flops | bytes accessed | tf_op | source)
XLA Modules:
  0.0 349.4 jit_solution(12880504687697954196)
XLA Ops:
  6.5 5.3 %collective-permute-start = (bf16[4,64,1024]{2,1,0:T(8,128)(2,1)}, bf16[4,64,1024]{2,1,0:T(8,128)(2,1)S(1)}, u32[]{:S(2)}, u32[]{:S(2)}) collective-permute-start(bf16[4,64,1024]{2,1,0:T(8,128)(2,1)} %param.13), channel_id=1, source_target_pairs={{0,16},{16,32},{32,48},{48,64},{64,80},{80,96},{96,112},{1,17},{17... | collective-permute-start | bytes 1572872 | tf_op jit(solution)/shard_map/ppermute | solution.py:14
  12.8 10.5 %collective-permute-done = bf16[4,64,1024]{2,1,0:T(8,128)(2,1)S(1)} collective-permute-done((bf16[4,64,1024]{2,1,0:T(8,128)(2,1)}, bf16[4,64,1024]{2,1,0:T(8,128)(2,1)S(1)}, u32[]{:S(2)}, u32[]{:S(2)}) %collective-permute-start) | collective-permute-done | bytes 524320 | tf_op jit(solution)/shard_map/ppermute | solution.py:14
  26.9 15.0 %fusion.53 = (f32[256]{0:T(256)S(1)}, bf16[256,1024]{1,0:T(8,128)(2,1)}) fusion(bf16[3072,1024]{1,0:T(8,128)(2,1)} %param.19, bf16[256,1024]{1,0:T(8,128)(2,1)S(1)} %fusion.63, bf16[1024,3072]{1,0:T(8,128)(2,1)} %param.18, bf16[256,1024]{1,0:T(8,128)(2,1)S(1)} %bitcast.73), kind=kOutput, calls=%fused_computation.70 | convolution fusion | flops 3273916160 | bytes 14156800 | tf_op jit(solution)/shard_map/dot_general | solution.py:103
  41.9 1.8 convolution_convert_fusion.2
  45.4 18.3 %all_to_all.68 = bf16[8,2,16384]{2,1,0:T(2,128)(2,1)S(1)} all-to-all(bf16[8,2,16384]{2,1,0:T(2,128)(2,1)S(1)} %reshape.198), channel_id=1, replica_groups=mesh['tm'=8,'agent'=16] {'tm'}, dimensions={0} | all-to-all | bytes 1048576 | tf_op jit(solution)/shard_map/all_to_all | solution.py:127
  65.7 2.4 convolution_convert_fusion
  70.3 3.5 all-to-all-start.2
  73.8 2.3 convolution_convert_fusion.1
  78.5 12.0 %all-to-all-done.2 = bf16[8,2,16384]{2,1,0:T(2,128)(2,1)S(1)} async-done(((bf16[8,2,16384]{2,1,0:T(2,128)(2,1)}), bf16[8,2,16384]{2,1,0:T(2,128)(2,1)S(1)}, u32[]{:S(2)}, u32[]{:S(2)}) %all-to-all-start.2) | async-done | bytes 524320 | tf_op jit(solution)/shard_map/all_to_all | solution.py:126
  90.5 3.5 %all-to-all-start.1 = ((bf16[8,2,16384]{2,1,0:T(2,128)(2,1)}), bf16[8,2,16384]{2,1,0:T(2,128)(2,1)S(1)}, u32[]{:S(2)}, u32[]{:S(2)}) async-start(bf16[8,2,16384]{2,1,0:T(2,128)(2,1)} %reshape.202), calls=%async_computation.1 | async-start | bytes 1048576 | tf_op jit(solution)/shard_map/all_to_all | solution.py:125
  95.2 15.1 %all-to-all-done.1 = bf16[8,2,16384]{2,1,0:T(2,128)(2,1)S(1)} async-done(((bf16[8,2,16384]{2,1,0:T(2,128)(2,1)}), bf16[8,2,16384]{2,1,0:T(2,128)(2,1)S(1)}, u32[]{:S(2)}, u32[]{:S(2)}) %all-to-all-start.1) | async-done | bytes 524320 | tf_op jit(solution)/shard_map/all_to_all | solution.py:125
  110.3 5.4 %stack.5 = bf16[16,32,64,128]{3,2,1,0:T(8,128)(2,1)} broadcast(bf16[32,64,128]{2,1,0:T(8,128)(2,1)S(1)} %bitcast.74), dimensions={1,2,3} | broadcast | bytes 8912896 | tf_op jit(solution)/shard_map/stack | solution.py:135
  115.7 6.9 %all-to-all-start.3 = ((bf16[16,32,64,128]{3,2,1,0:T(8,128)(2,1)}), bf16[16,32,64,128]{3,2,1,0:T(8,128)(2,1)}, u32[]{:S(2)}, u32[]{:S(2)}) async-start(bf16[16,32,64,128]{3,2,1,0:T(8,128)(2,1)} %stack.5), calls=%async_computation.3 | async-start | bytes 16777216 | tf_op jit(solution)/shard_map/all_to_all | solution.py:135
  124.2 99.1 %all-reduce.2 = (s32[1024]{0:T(1024)S(1)}, s32[1024]{0:T(1024)S(1)}) all-reduce(s32[1024]{0:T(1024)S(1)} %dynamic-update-slice, s32[1024]{0:T(1024)S(1)} %dynamic-update-slice.1), channel_id=2, replica_groups=mesh['tm'=8,'agent'=16] {'agent'}, use_global_device_ids=true, to_apply=%add | all-reduce | flops 2048 | bytes 16384
  224.9 3.0 reshape.203
  229.1 2.4 reshape.177
  231.6 18.7 %copy.34 = bf16[32,16,64,128]{2,1,3,0:T(8,128)(2,1)} copy(bf16[32,16,64,128]{3,2,0,1:T(8,128)(2,1)} %bitcast.21) | data formatting | bytes 16777216 | tf_op jit(solution)/shard_map/reshape | solution.py:135
  250.3 22.6 %reshape_reshape.3 = bf16[32,1024,2,64]{1,3,2,0:T(8,128)(2,1)} reshape(bf16[32,16,64,128]{2,1,3,0:T(8,128)(2,1)} %copy.34) | data formatting | bytes 16777216 | tf_op jit(solution)/shard_map/reshape;reshape | solution.py:38
  272.9 10.1 %fusion = (f32[32,2,64]{2,1,0:T(2,128)S(1)}, f32[32,2,64,1024]{3,2,1,0:T(8,128)}) fusion(pred[32,64,1024]{2,1,0:T(8,128)(4,1)S(1)} %and_or_fusion, bf16[32,1024,2,64]{1,3,2,0:T(8,128)(2,1)} %reshape_reshape.3, bf16[32,64,2,64]{3,2,1,0:T(2,128)(2,1)S(1)} %reshape.177), kind=kOutput, calls=%fused_computation.3 | convolution fusion | flops 549449728 | bytes 27803648 | tf_op jit(solution)/shard_map/sahd,sbhd->shab/dot_general | solution.py:41
  283.0 8.8 %convert_reduce_fusion = f32[32,2,64]{2,1,0:T(2,128)S(1)} fusion(f32[32,2,64]{2,1,0:T(2,128)S(1)} %broadcast_maximum_fusion, f32[32,2,64,1024]{3,2,1,0:T(8,128)} %get-tuple-element.19, pred[32,64,1024]{2,1,0:T(8,128)(4,1)S(1)} %and_or_fusion), kind=kLoop, calls=%fused_computation | loop fusion | flops 29356032 | bytes 18907136 | tf_op jit(solution)/shard_map/reduce_sum | solution.py:54
  291.8 12.2 %copy.27 = bf16[32,1024,128]{1,2,0:T(8,128)(2,1)} copy(bf16[32,1024,128]{2,0,1:T(8,128)(2,1)} %all-gather.4.cloned.1.call-done) | data formatting | bytes 16777216 | tf_op jit(solution)/shard_map/all_gather | solution.py:136
  304.1 11.7 %fusion.13 = bf16[32,64,2,64]{1,3,2,0:T(8,128)(2,1)} fusion(bf16[32,1024,2,64]{1,3,2,0:T(8,128)(2,1)} %bitcast.66, f32[32,64,2]{1,2,0:T(2,128)S(1)} %bitcast.83, f32[32,2,64,1024]{3,2,1,0:T(8,128)} %get-tuple-element.19, f32[32,2,64]{2,1,0:T(2,128)S(1)} %broadcast_maximum_fusion, pred[32,64,1024]{2,1,0:T(8,128)(4,1)S(1)} %and_or_fusion), kind=kOutput, calls=%fused_computation.29 | convolution fusion | flops 558366720 | bytes 27820032 | tf_op jit(solution)/shard_map/shab,sbhd->sahd/dot_general | solution.py:55
  317.5 21.5 %all_to_all.69 = bf16[32,64,128]{2,1,0:T(8,128)(2,1)S(1)} all-to-all(bf16[32,64,128]{2,1,0:T(8,128)(2,1)S(1)} %copy.36), channel_id=1, replica_groups=mesh['tm'=8,'agent'=16] {'tm'}, dimensions={0} | all-to-all | bytes 1048576 | tf_op jit(solution)/shard_map/all_to_all | solution.py:143
  339.4 3.1 fusion.49
  (57 shorter events, 19.8 us)
Async XLA Ops:
  6.5 35.4 %copy-start = (bf16[1024,1024]{1,0:T(8,128)(2,1)S(1)}, bf16[1024,1024]{1,0:T(8,128)(2,1)}, u32[]{:S(2)}) copy-start(bf16[1024,1024]{1,0:T(8,128)(2,1)} %param.22) | copy-start | bytes 6291460
  6.5 19.4 %copy-start.2 = (bf16[4,64,1024]{2,1,0:T(8,128)(2,1)S(1)}, bf16[4,64,1024]{2,1,0:T(8,128)(2,1)}, u32[]{:S(2)}) copy-start(bf16[4,64,1024]{2,1,0:T(8,128)(2,1)} %param.13) | copy-start | bytes 1572868
  6.5 285.3 %all-gather.4.cloned.1.call-start = ((), (), s32[]{:S(2)}) async-start(), calls=%async_computation.5 | async-start | bytes 8912896 | tf_op jit(solution)/shard_map/all_gather | solution.py:136
  6.5 16.8 %collective-permute-start = (bf16[4,64,1024]{2,1,0:T(8,128)(2,1)}, bf16[4,64,1024]{2,1,0:T(8,128)(2,1)S(1)}, u32[]{:S(2)}, u32[]{:S(2)}) collective-permute-start(bf16[4,64,1024]{2,1,0:T(8,128)(2,1)} %param.13), channel_id=1, source_target_pairs={{0,16},{16,32},{32,48},{48,64},{64,80},{80,96},{96,112},{1,17},{17... | collective-permute-start | bytes 1572872 | tf_op jit(solution)/shard_map/ppermute | solution.py:14
  26.0 0.7 copy-start.4
  26.9 15.1 %copy-start.6 = (f32[1024]{0:T(1024)S(1)}, f32[1024]{0:T(1024)}, u32[]{:S(2)}) copy-start(f32[1024]{0:T(1024)} %param.17) | copy-start | bytes 12292
  44.6 21.1 %copy-start.9 = (bf16[256,1024]{1,0:T(8,128)(2,1)S(1)}, bf16[256,1024]{1,0:T(8,128)(2,1)}, u32[]{:S(2)}) copy-start(bf16[256,1024]{1,0:T(8,128)(2,1)} %get-tuple-element.17) | copy-start | bytes 1572868
  70.3 20.1 %all-to-all-start.2 = ((bf16[8,2,16384]{2,1,0:T(2,128)(2,1)}), bf16[8,2,16384]{2,1,0:T(2,128)(2,1)S(1)}, u32[]{:S(2)}, u32[]{:S(2)}) async-start(bf16[8,2,16384]{2,1,0:T(2,128)(2,1)} %reshape.200), calls=%async_computation.2 | async-start | bytes 1048576 | tf_op jit(solution)/shard_map/all_to_all | solution.py:126
  90.5 19.9 %all-to-all-start.1 = ((bf16[8,2,16384]{2,1,0:T(2,128)(2,1)}), bf16[8,2,16384]{2,1,0:T(2,128)(2,1)S(1)}, u32[]{:S(2)}, u32[]{:S(2)}) async-start(bf16[8,2,16384]{2,1,0:T(2,128)(2,1)} %reshape.202), calls=%async_computation.1 | async-start | bytes 1048576 | tf_op jit(solution)/shard_map/all_to_all | solution.py:125
  110.3 5.4 %copy-start.3 = (bf16[8,2,16384]{2,1,0:T(2,128)(2,1)}, bf16[8,2,16384]{2,1,0:T(2,128)(2,1)S(1)}, u32[]{:S(2)}) copy-start(bf16[8,2,16384]{2,1,0:T(2,128)(2,1)S(1)} %all-to-all-done.1) | copy-start | bytes 1572868
  115.7 6.9 %copy-start.8 = (u32[128]{0:T(128)S(1)}, u32[128]{0:T(128)}, u32[]{:S(2)}) copy-start(u32[128]{0:T(128)} %constant.80) | copy-start | bytes 1540
  115.7 8.0 %copy-start.5 = (s32[64]{0:T(128)S(1)}, s32[64]{0:T(128)}, u32[]{:S(2)}) copy-start(s32[64]{0:T(128)} %param.24) | copy-start | bytes 772
  115.7 8.3 %copy-start.7 = (s32[64]{0:T(128)S(1)}, s32[64]{0:T(128)}, u32[]{:S(2)}) copy-start(s32[64]{0:T(128)} %param.25) | copy-start | bytes 772
  115.7 115.9 %all-to-all-start.3 = ((bf16[16,32,64,128]{3,2,1,0:T(8,128)(2,1)}), bf16[16,32,64,128]{3,2,1,0:T(8,128)(2,1)}, u32[]{:S(2)}, u32[]{:S(2)}) async-start(bf16[16,32,64,128]{3,2,1,0:T(8,128)(2,1)} %stack.5), calls=%async_computation.3 | async-start | bytes 16777216 | tf_op jit(solution)/shard_map/all_to_all | solution.py:135
  315.8 23.6 %copy-start.10 = (bf16[256,1024]{1,0:T(8,128)(2,1)S(1)}, bf16[256,1024]{1,0:T(8,128)(2,1)}, u32[]{:S(2)}) copy-start(bf16[256,1024]{1,0:T(8,128)(2,1)} %get-tuple-element.17) | copy-start | bytes 1572868
  315.8 26.7 %copy-start.1 = (bf16[1024,1024]{1,0:T(8,128)(2,1)S(1)}, bf16[1024,1024]{1,0:T(8,128)(2,1)}, u32[]{:S(2)}) copy-start(bf16[1024,1024]{1,0:T(8,128)(2,1)} %param.22) | copy-start | bytes 6291460
Sparse Core Ops, SparseCore 0:
  65.8 59.2 all-gather.3
